TPU v7x, 32 devices: a whole 2x2x4 slice. The times are simulated.
32 devices in a mesh: prow: 8 (over y, x, core), pcol: 4 (over z).
Axes of the slice: x: 2, y: 2, z: 4, core: 2. Of those that a mesh axis runs over, the one named last changes fastest.
Arguments:
- inverse_trailing: bfloat16 [18432, 18432], P('prow', 'pcol'), may hold values from -6 to 6
- panel: bfloat16 [18432, 256], P('prow'), may hold values from -0.0625 to 0.0625
- supernode_inverse: float32 [256, 256], replicated, may hold values from -6 to 6
- block_live: int32 [72], replicated, may hold values from 0 to 1, as said below
Outputs:
- column_inverse: float32 [18432, 256], P('prow')
- diagonal_inverse: float32 [256, 256], replicated
Inputs may be any that keep to these rules, and one draw needn't show every extreme that they name: Each aligned group of 9 consecutive block rows (the rows of one index of prow) holds at least one block row with block_live 1.
All inputs are finite; a program needn't handle non-finite values.
Results may differ from a plain program's by a relative error of at most 0.0003.
Values may be sent and summed in bfloat16 or wider, within the bound.
No kernel may reach another device: no remote copies, remote signals or barrier semaphores. Data moves between devices by JAX's collectives and lax.ppermute only.
A program may use at most 128 MiB of HBM per device.

v0:
```python
import jax
import jax.numpy as jnp
from jax import lax
from jax.sharding import PartitionSpec as P


def from_root(block, axis, source):
    block = jnp.where(lax.axis_index(axis) == source, block, jnp.zeros_like(block))
    return lax.psum(block, axis)


def per_device(inverse_trailing, panel, supernode_inverse, block_live):
    rows_dev = panel.shape[0]
    width = panel.shape[1]
    col_count = inverse_trailing.shape[1]
    ratio = lax.axis_size("prow") // lax.axis_size("pcol")
    row_index = lax.axis_index("prow")
    col_index = lax.axis_index("pcol")
    live_all = jnp.repeat(block_live, width)
    col_live = lax.dynamic_slice_in_dim(live_all, col_index * col_count, col_count).astype(
        jnp.float32
    )
    row_live = lax.dynamic_slice_in_dim(live_all, row_index * rows_dev, rows_dev).astype(
        jnp.float32
    )
    partial_sum = jnp.zeros((rows_dev, width), jnp.float32)
    for half in range(ratio):
        received = from_root(panel, "prow", col_index * ratio + half)
        half_live = col_live[half * rows_dev : (half + 1) * rows_dev]
        masked_half = (received.astype(jnp.float32) * half_live[:, None]).astype(jnp.bfloat16)
        tile_cols = inverse_trailing[:, half * rows_dev : (half + 1) * rows_dev]
        partial_sum = partial_sum + jnp.dot(
            tile_cols, masked_half, preferred_element_type=jnp.float32
        )
    local_panel = panel.astype(jnp.float32) * row_live[:, None]
    contract_rows = (((0,), (0,)), ((), ()))
    total = lax.psum(partial_sum, "pcol")
    column_inverse = -total * row_live[:, None]
    term = lax.dot_general(
        local_panel, column_inverse, contract_rows, precision=lax.Precision.HIGHEST
    )
    diag_total = lax.psum(term, "prow")
    diagonal_inverse = supernode_inverse - diag_total
    return (column_inverse, diagonal_inverse)


def solution(mesh):
    in_specs = (P("prow", "pcol"), P("prow", None), P(), P())
    out_specs = (P("prow", None), P())
    return jax.shard_map(
        per_device, mesh=mesh, in_specs=in_specs, out_specs=out_specs, check_vma=False
    )
```

profile of v0, /device:TPU:0, one launch (start us, length us, event | category | flops | bytes accessed | tf_op | source)
XLA Modules:
  0.0 254.0 jit_solution(5009432006979550034)
XLA Ops:
  7.2 0.0 copy-start
  7.2 0.0 all-reduce.9.cloned.1.call-start
  7.2 2.8 %broadcast_select_fusion.1 = (bf16[2304,256]{1,0:T(8,128)(2,1)}, bf16[2304,256]{1,0:T(8,128)(2,1)}) fusion(bf16[2304,256]{1,0:T(8,128)(2,1)} %param.5, pred[]{:T(512)S(6)} %eq.6, pred[]{:T(512)S(6)} %eq.7), kind=kLoop, calls=%fused_computation.16 | loop fusion | flops 1179648 | bytes 3538946 | tf_op jit(solution)/shard_map/jit(_where)/select_n | solution.py:8
  10.1 0.0 all-reduce.9.cloned.1.call-update
  10.1 0.0 all-reduce.5.cloned.1.call-start
  10.2 0.0 copy-done
  10.2 0.1 broadcast_bitcast_fusion
  10.3 0.1 dynamic-slice_convert_fusion
  10.4 67.3 %all-reduce.9.cloned.1.call-done = (bf16[2304,256]{1,0:T(8,128)(2,1)}, bf16[2304,256]{1,0:T(8,128)(2,1)}) async-done(((bf16[2304,256]{1,0:T(8,128)(2,1)}, bf16[2304,256]{1,0:T(8,128)(2,1)}), (bf16[2304,256]{1,0:T(8,128)(2,1)}, bf16[2304,256]{1,0:T(8,128)(2,1)})) %all-reduce.9.cloned.1.call-update) | async-done | bytes 2359312 | tf_op jit(solution)/shard_map/psum | solution.py:9
  77.6 0.0 copy-start.3
  77.7 7.3 %fusion = f32[256,2304]{1,0:T(8,128)S(1)} fusion(bf16[2304,4608]{1,0:T(8,128)(2,1)} %param.4, bf16[2304,256]{1,0:T(8,128)(2,1)} %get-tuple-element.4, f32[2304]{0:T(1024)S(1)} %get-tuple-element.9), kind=kOutput, calls=%fused_computation | convolution fusion | flops 2719678464 | bytes 14164992 | tf_op jit(solution)/shard_map/dot_general | solution.py:32
  85.0 0.0 copy-done.3
  85.0 8.9 %fusion.7 = f32[2304,256]{0,1:T(8,128)} fusion(f32[256,2304]{1,0:T(8,128)S(1)} %fusion, bf16[2304,4608]{1,0:T(8,128)(2,1)} %param.4, bf16[2304,256]{1,0:T(8,128)(2,1)S(1)} %copy-done.3, f32[2304]{0:T(1024)S(1)} %get-tuple-element.8), kind=kOutput, calls=%fused_computation.5 | convolution fusion | flops 2720268288 | bytes 16524288 | tf_op jit(solution)/shard_map/dot_general | solution.py:32
  93.9 0.0 copy-start.1
  93.9 0.0 all-reduce.5.cloned.1.call-update
  93.9 0.0 all-reduce.7.cloned.1.call-start
  94.0 1.2 copy-done.1
  95.2 0.7 copy.6
  95.9 0.1 dynamic-slice_convert_fusion.1
  96.0 92.0 %all-reduce.5.cloned.1.call-done = f32[2304,256]{0,1:T(8,128)} async-done(((f32[2304,256]{0,1:T(8,128)}), f32[2304,256]{0,1:T(8,128)}) %all-reduce.5.cloned.1.call-update) | async-done | bytes 2359312 | tf_op jit(solution)/shard_map/psum | solution.py:37
  188.0 4.7 %fusion.10 = f32[256,256]{1,0:T(8,128)} fusion(bf16[2304,256]{0,1:T(8,128)(2,1)S(1)} %copy.6, f32[2304]{0:T(1024)S(1)} %dynamic-slice_convert_fusion.1, f32[2304,256]{0,1:T(8,128)} %all-reduce.5.cloned.1.call-done), kind=kOutput, calls=%fused_computation.6 | convolution fusion | flops 1814298624 | bytes 3810304 | tf_op jit(solution)/shard_map/dot_general | solution.py:39
  192.7 0.0 all-reduce.7.cloned.1.call-update
  192.7 1.8 negate_multiply_fusion
  194.6 0.0 copy-start.2
  194.6 2.0 copy.7
  196.5 49.3 %all-reduce.7.cloned.1.call-done = f32[256,256]{1,0:T(8,128)} async-done(((f32[256,256]{1,0:T(8,128)}), f32[256,256]{1,0:T(8,128)}) %all-reduce.7.cloned.1.call-update) | async-done | bytes 262160 | tf_op jit(solution)/shard_map/psum | solution.py:42
  245.8 0.0 copy-done.2
  245.8 1.7 sub.3
  (2 shorter events, 0.0 us)
Async XLA Ops:
  7.2 3.0 %copy-start = (s32[72]{0:T(128)S(1)}, s32[72]{0:T(128)}, u32[]{:S(2)}) copy-start(s32[72]{0:T(128)} %param.7) | copy-start | bytes 868
  7.2 70.5 %all-reduce.9.cloned.1.call-start = ((), (), s32[]{:S(2)}) async-start(), calls=%async_computation.2 | async-start | bytes 4718592 | tf_op jit(solution)/shard_map/psum | solution.py:9
  10.1 177.9 %all-reduce.5.cloned.1.call-start = ((), (), s32[]{:S(2)}) async-start(), calls=%async_computation | async-start | bytes 4718592 | tf_op jit(solution)/shard_map/psum | solution.py:37
  77.6 7.3 %copy-start.3 = (bf16[2304,256]{1,0:T(8,128)(2,1)S(1)}, bf16[2304,256]{1,0:T(8,128)(2,1)}, u32[]{:S(2)}) copy-start(bf16[2304,256]{1,0:T(8,128)(2,1)} %get-tuple-element.5) | copy-start | bytes 3538948
  93.9 1.3 copy-start.1
  93.9 151.9 %all-reduce.7.cloned.1.call-start = ((), (), s32[]{:S(2)}) async-start(), calls=%async_computation.1 | async-start | bytes 524288 | tf_op jit(solution)/shard_map/psum | solution.py:42
  194.6 51.2 %copy-start.2 = (f32[256,256]{1,0:T(8,128)S(1)}, f32[256,256]{1,0:T(8,128)}, u32[]{:S(2)}) copy-start(f32[256,256]{1,0:T(8,128)} %param.6) | copy-start | bytes 786436
Sparse Core Ops, SparseCore 0:
  11.9 65.7 all-reduce.8
  94.0 93.9 all-reduce.4
  192.9 52.9 all-reduce.6
where the time goes:
time: 254 us
  waiting for transfers between devices  209 us (82%)
  matrix products  20.9 us (8%)
  between operations  13.8 us (5%)
  other arithmetic  6.55 us (3%)
  local copies, waits for them, and re-layouts  4.01 us (2%)
    psum x1, waiting for transfers between devices, per_device(): total = lax.psum(partial_sum, 'pcol')  92 us
    psum x1, waiting for transfers between devices, from_root(): return lax.psum(block, axis)  67.3 us
    psum x1, waiting for transfers between devices, per_device(): diag_total = lax.psum(term, 'prow')  49.3 us
    dot_general x2, matrix products, per_device(): jnp.dot(tile_cols, masked_half, preferred_element_type=jnp.float32)  16.2 us
  transfers between devices with their start and end apart: 3, of which 3 were waited for; matrix products, arithmetic and copies ran while one was open for 2% of the time, Pallas kernels for 0%

commit v1 on v0

--- a/solution.py
+++ b/solution.py
@@ -39,7 +39,7 @@
     term = lax.dot_general(
         local_panel, column_inverse, contract_rows, precision=lax.Precision.HIGHEST
     )
-    diag_total = lax.psum(term, "prow")
+    diag_total = jnp.sum(lax.all_gather(term, "prow"), axis=0)
     diagonal_inverse = supernode_inverse - diag_total
     return (column_inverse, diagonal_inverse)
 

time: 254 us -> 229 us (0.902)
  waiting for transfers between devices: 209 us -> 183 us
    psum x1 -> x0, waiting for transfers between devices: 49.3 us -> none  [per_device(): diag_total = lax.psum(term, 'prow')]
    all_gather x0 -> x1, waiting for transfers between devices: none -> 23.2 us  [per_device(): diag_total = jnp.sum(lax.all_gather(term, 'prow'), axis=0)]
where the time goes in v1:
time: 229 us
  waiting for transfers between devices  183 us (80%)
  matrix products  20.9 us (9%)
  between operations  13.8 us (6%)
  other arithmetic  7.34 us (3%)
  local copies, waits for them, and re-layouts  4 us (2%)
    psum x1, waiting for transfers between devices, per_device(): total = lax.psum(partial_sum, 'pcol')  92 us
    psum x1, waiting for transfers between devices, from_root(): return lax.psum(block, axis)  67.3 us
    all_gather x1, waiting for transfers between devices, per_device(): diag_total = jnp.sum(lax.all_gather(term, 'prow'), axis=0)  23.2 us
    dot_general x2, matrix products, per_device(): jnp.dot(tile_cols, masked_half, preferred_element_type=jnp.float32)  16.2 us
    dot_general x1, matrix products, per_device(): lax.dot_general(local_panel, column_inverse, contract_rows, precision=lax...  4.7 us
  transfers between devices with their start and end apart: 3, of which 3 were waited for; matrix products, arithmetic and copies ran while one was open for 2% of the time, Pallas kernels for 0%

profile of v1, /device:TPU:0, one launch (start us, length us, event | category | flops | bytes accessed | tf_op | source)
XLA Modules:
  0.0 228.7 jit_solution(10002361908651925015)
XLA Ops:
  7.2 0.0 copy-start
  7.2 0.0 all-reduce.6.cloned.1.call-start
  7.2 2.8 %broadcast_select_fusion.1 = (bf16[2304,256]{1,0:T(8,128)(2,1)}, bf16[2304,256]{1,0:T(8,128)(2,1)}) fusion(bf16[2304,256]{1,0:T(8,128)(2,1)} %param.5, pred[]{:T(512)S(6)} %eq.6, pred[]{:T(512)S(6)} %eq.7), kind=kLoop, calls=%fused_computation.16 | loop fusion | flops 1179648 | bytes 3538946 | tf_op jit(solution)/shard_map/jit(_where)/select_n | solution.py:8
  10.1 0.0 all-reduce.6.cloned.1.call-update
  10.1 0.0 all-reduce.4.cloned.1.call-start
  10.2 0.0 copy-done
  10.2 0.1 broadcast_bitcast_fusion
  10.3 0.1 dynamic-slice_convert_fusion
  10.4 67.3 %all-reduce.6.cloned.1.call-done = (bf16[2304,256]{1,0:T(8,128)(2,1)}, bf16[2304,256]{1,0:T(8,128)(2,1)}) async-done(((bf16[2304,256]{1,0:T(8,128)(2,1)}, bf16[2304,256]{1,0:T(8,128)(2,1)}), (bf16[2304,256]{1,0:T(8,128)(2,1)}, bf16[2304,256]{1,0:T(8,128)(2,1)})) %all-reduce.6.cloned.1.call-update) | async-done | bytes 2359312 | tf_op jit(solution)/shard_map/psum | solution.py:9
  77.6 0.0 copy-start.3
  77.7 7.3 %fusion = f32[256,2304]{1,0:T(8,128)S(1)} fusion(bf16[2304,4608]{1,0:T(8,128)(2,1)} %param.4, bf16[2304,256]{1,0:T(8,128)(2,1)} %get-tuple-element.4, f32[2304]{0:T(1024)S(1)} %get-tuple-element.9), kind=kOutput, calls=%fused_computation | convolution fusion | flops 2719678464 | bytes 14164992 | tf_op jit(solution)/shard_map/dot_general | solution.py:32
  85.0 0.0 copy-done.3
  85.0 8.9 %fusion.7 = f32[2304,256]{0,1:T(8,128)} fusion(f32[256,2304]{1,0:T(8,128)S(1)} %fusion, bf16[2304,4608]{1,0:T(8,128)(2,1)} %param.4, bf16[2304,256]{1,0:T(8,128)(2,1)S(1)} %copy-done.3, f32[2304]{0:T(1024)S(1)} %get-tuple-element.8), kind=kOutput, calls=%fused_computation.5 | convolution fusion | flops 2720268288 | bytes 16524288 | tf_op jit(solution)/shard_map/dot_general | solution.py:32
  93.9 0.0 copy-start.1
  93.9 0.0 all-reduce.4.cloned.1.call-update
  93.9 0.0 all-gather.3.cloned.1.call-start
  94.0 1.2 copy-done.1
  95.2 0.7 copy.6
  95.9 0.1 dynamic-slice_convert_fusion.1
  96.0 92.0 %all-reduce.4.cloned.1.call-done = f32[2304,256]{0,1:T(8,128)} async-done(((f32[2304,256]{0,1:T(8,128)}), f32[2304,256]{0,1:T(8,128)}) %all-reduce.4.cloned.1.call-update) | async-done | bytes 2359312 | tf_op jit(solution)/shard_map/psum | solution.py:37
  188.0 4.7 %fusion.10 = f32[256,256]{1,0:T(8,128)} fusion(bf16[2304,256]{0,1:T(8,128)(2,1)S(1)} %copy.6, f32[2304]{0:T(1024)S(1)} %dynamic-slice_convert_fusion.1, f32[2304,256]{0,1:T(8,128)} %all-reduce.4.cloned.1.call-done), kind=kOutput, calls=%fused_computation.6 | convolution fusion | flops 1814298624 | bytes 3810304 | tf_op jit(solution)/shard_map/dot_general | solution.py:39
  192.7 0.0 all-gather.3.cloned.1.call-update
  192.7 1.8 negate_multiply_fusion
  194.6 2.0 copy.7
  196.5 0.0 copy-start.2
  196.5 23.2 %all-gather.3.cloned.1.call-done = f32[2048,256]{1,0:T(8,128)} async-done(((f32[256,256]{1,0:T(8,128)}), f32[2048,256]{1,0:T(8,128)}) %all-gather.3.cloned.1.call-update) | async-done | bytes 2097168 | tf_op jit(solution)/shard_map/all_gather | solution.py:42
  219.7 1.8 reduce_sum.9
  221.5 0.0 copy-done.2
  221.5 0.7 sub.3
  (2 shorter events, 0.0 us)
Async XLA Ops:
  7.2 3.0 %copy-start = (s32[72]{0:T(128)S(1)}, s32[72]{0:T(128)}, u32[]{:S(2)}) copy-start(s32[72]{0:T(128)} %param.7) | copy-start | bytes 868
  7.2 70.5 %all-reduce.6.cloned.1.call-start = ((), (), s32[]{:S(2)}) async-start(), calls=%async_computation.2 | async-start | bytes 4718592 | tf_op jit(solution)/shard_map/psum | solution.py:9
  10.1 177.9 %all-reduce.4.cloned.1.call-start = ((), (), s32[]{:S(2)}) async-start(), calls=%async_computation | async-start | bytes 4718592 | tf_op jit(solution)/shard_map/psum | solution.py:37
  77.6 7.3 %copy-start.3 = (bf16[2304,256]{1,0:T(8,128)(2,1)S(1)}, bf16[2304,256]{1,0:T(8,128)(2,1)}, u32[]{:S(2)}) copy-start(bf16[2304,256]{1,0:T(8,128)(2,1)} %get-tuple-element.5) | copy-start | bytes 3538948
  93.9 1.3 copy-start.1
  93.9 125.8 %all-gather.3.cloned.1.call-start = ((), (), s32[]{:S(2)}) async-start(), calls=%async_computation.1 | async-start | bytes 2359296 | tf_op jit(solution)/shard_map/all_gather | solution.py:42
  196.5 24.9 %copy-start.2 = (f32[256,256]{1,0:T(8,128)S(1)}, f32[256,256]{1,0:T(8,128)}, u32[]{:S(2)}) copy-start(f32[256,256]{1,0:T(8,128)} %param.6) | copy-start | bytes 786436
Sparse Core Ops, SparseCore 0:
  11.9 65.7 all-reduce.5
  94.0 93.9 all-reduce.3
  192.9 26.7 all-gather.2
